TPU v7x, 512 devices: a whole 4x4x16 slice. The times are simulated.
512 devices in a mesh: roll: 64 (over x, z_hi, y, core), kv: 8 (over z_lo).
Axes of the slice: x: 4, y: 4, z: 16 (z_hi: 2, z_lo: 8; z = z_hi * 8 + z_lo), core: 2. Of those that a mesh axis runs over, the one named last changes fastest.
Arguments:
- queries: bfloat16 [64, 4, 2048], P('roll', None, 'kv'), may hold values from -8 to 8
- prompt_cache: bfloat16 [4, 16384, 1024], P(None, 'roll', 'kv'), may hold values from -4 to 4
- gen_cache: bfloat16 [64, 128, 1024], P('roll', None, 'kv'), may hold values from -4 to 4
- gen_lengths: int32 [64], P('roll'), may hold values from 1 to 128, 4096 in all
- new_kv: bfloat16 [64, 4, 1024], P('roll', None, 'kv'), may hold values from -4 to 4
- w_out: bfloat16 [2048, 2880], P('kv'), may hold values from -3 to 3
- residual: bfloat16 [64, 4, 2880], P('roll', None, 'kv'), may hold values from -10 to 10
- norm_gain: float32 [2880], P('kv'), may hold values from 0.5 to 1.5
- w_gate: bfloat16 [64, 2880, 1440], P('roll', None, 'kv'), may hold values from -0.109375 to 0.109375
- w_up: bfloat16 [64, 2880, 1440], P('roll', None, 'kv'), may hold values from -0.109375 to 0.109375
- w_down: bfloat16 [64, 1440, 2880], P('roll', 'kv'), may hold values from -0.15625 to 0.15625
- expert_ids: int32 [64, 4, 4], replicated, may hold values from 0 to 63, all different within a row; in each aligned block of 256 rows (0 to 255, 256 to 511, ..., all dimensions but the last counted through in order) at most 48 rows name the same one
- route_weights: float32 [64, 4, 4], replicated, may hold values from 0.05 to 0.5
Outputs:
- layer_out: bfloat16 [64, 4, 2880], P('roll', None, 'kv')
Inputs may be any that keep to these rules, and one draw needn't show every extreme that they name: `expert_ids`: each row names 4 different experts; over all rows no expert is named more than 48 times, and one expert exactly 48 times. `gen_lengths`: the longest is exactly 128.
All inputs are finite; a program needn't handle non-finite values. No bound on the sum of `gen_lengths` on one device may be relied on, other than what follows from the above.
Results may differ from a plain program's by a relative error of at most 0.014.
Values may be sent and summed in bfloat16 or wider, within the bound.
A program may use at most 128 MiB of HBM per device.

v0:
```python
import jax
import jax.numpy as jnp
from jax import lax
from jax.sharding import PartitionSpec as P

D = 2880
HEAD = 64
TOPK = 4
MOSTE = 48


def merged(x, axis, combine):
    everything = jax.tree.map(lambda part: lax.all_gather(part, axis), x)
    initial = jax.tree.map(lambda part: part[0], everything)

    def hop(k, so_far):
        return combine(so_far, jax.tree.map(lambda part: part[k], everything))

    return lax.fori_loop(1, lax.axis_size(axis), hop, initial)


def merge_pair(left_part, right_part):
    maxima = jnp.maximum(left_part[0], right_part[0])
    left_factor = jnp.exp(left_part[0] - maxima)
    right_factor = jnp.exp(right_part[0] - maxima)
    totals = left_part[1] * left_factor + right_part[1] * right_factor
    accumulated = left_part[2] * left_factor[..., None] + right_part[2] * right_factor[..., None]
    return (maxima, totals, accumulated)


def on_device(
    queries,
    prompt_cache,
    gen_cache,
    gen_lengths,
    new_kv,
    w_out,
    residual,
    norm_gain,
    w_gate,
    w_up,
    w_down,
    expert_ids,
    route_weights,
):
    highest = lax.Precision.HIGHEST
    samp_local, step_count, query_width = queries.shape
    prompt_count, prompt_local, kv_width = prompt_cache.shape
    kv_local = kv_width // (2 * HEAD)
    per_group = query_width // (kv_local * HEAD)
    score_scale = HEAD ** (-0.5)
    roll_index = lax.axis_index("roll")
    everyone = lax.all_gather(queries, "roll", axis=0, tiled=True)
    group_size = everyone.shape[0] // prompt_count
    query_all = everyone.reshape(prompt_count, group_size, step_count, kv_local, per_group, HEAD)
    prompt_blocks = prompt_cache.reshape(prompt_count, prompt_local, kv_local, 2, HEAD)
    scores = (
        jnp.einsum(
            "pgtkrd,pnkd->pgtkrn",
            query_all,
            prompt_blocks[:, :, :, 0],
            preferred_element_type=jnp.float32,
        )
        * score_scale
    )
    maxima = jnp.max(scores, axis=-1)
    weights = jnp.exp(scores - maxima[..., None])
    totals = jnp.sum(weights, axis=-1)
    prompt_values = prompt_blocks[:, :, :, 1].astype(jnp.float32)
    accumulated = jnp.einsum("pgtkrn,pnkd->pgtkrd", weights, prompt_values, precision=highest)
    lead_shape = (prompt_count * group_size, step_count, kv_local, per_group)
    maxima = maxima.reshape(lead_shape)
    totals = totals.reshape(lead_shape)
    accumulated = accumulated.reshape(lead_shape + (HEAD,))
    maxima, totals, accumulated = merged((maxima, totals, accumulated), "roll", merge_pair)
    row_start = roll_index * samp_local
    maxima = lax.dynamic_slice_in_dim(maxima, row_start, samp_local, 0)
    totals = lax.dynamic_slice_in_dim(totals, row_start, samp_local, 0)
    accumulated = lax.dynamic_slice_in_dim(accumulated, row_start, samp_local, 0)
    own_query = queries.reshape(samp_local, step_count, kv_local, per_group, HEAD)
    gen_blocks = gen_cache.reshape(samp_local, -1, kv_local, 2, HEAD)
    gen_span = gen_blocks.shape[1]
    gen_scores = (
        jnp.einsum(
            "stkrd,snkd->stkrn",
            own_query,
            gen_blocks[:, :, :, 0],
            preferred_element_type=jnp.float32,
        )
        * score_scale
    )
    live_mask = jnp.arange(gen_span, dtype=jnp.int32)[None, :] < gen_lengths[:, None]
    gen_scores = jnp.where(live_mask[:, None, None, None, :], gen_scores, -jnp.inf)
    fresh_kv = new_kv.reshape(samp_local, step_count, kv_local, 2, HEAD)
    new_scores = (
        jnp.einsum(
            "stkrd,sukd->stkru", own_query, fresh_kv[:, :, :, 0], preferred_element_type=jnp.float32
        )
        * score_scale
    )
    causal = jnp.arange(step_count)[None, :] <= jnp.arange(step_count)[:, None]
    new_scores = jnp.where(causal[None, :, None, None, :], new_scores, -jnp.inf)
    overall = jnp.maximum(jnp.maximum(maxima, gen_scores.max(-1)), new_scores.max(-1))
    prompt_factor = jnp.exp(maxima - overall)
    gen_w = jnp.exp(gen_scores - overall[..., None])
    new_w = jnp.exp(new_scores - overall[..., None])
    denominator = totals * prompt_factor + gen_w.sum(-1) + new_w.sum(-1)
    numerator = accumulated * prompt_factor[..., None]
    numerator = numerator + jnp.einsum(
        "stkrn,snkd->stkrd", gen_w, gen_blocks[:, :, :, 1].astype(jnp.float32), precision=highest
    )
    numerator = numerator + jnp.einsum(
        "stkru,sukd->stkrd", new_w, fresh_kv[:, :, :, 1].astype(jnp.float32), precision=highest
    )
    local_rows = samp_local * step_count
    attended = (
        (numerator / denominator[..., None]).astype(jnp.bfloat16).reshape(local_rows, query_width)
    )
    projected = jnp.dot(attended, w_out, preferred_element_type=jnp.float32)
    projected = lax.psum_scatter(
        projected.astype(jnp.bfloat16), "kv", scatter_dimension=1, tiled=True
    ).astype(jnp.float32)
    residual_sum = residual.reshape(local_rows, -1).astype(jnp.float32) + projected
    squares = lax.psum(jnp.sum(residual_sum * residual_sum, axis=1), "kv")
    inverse = lax.rsqrt(squares / D + 1e-05)
    normed = (residual_sum * inverse[:, None] * norm_gain).astype(jnp.bfloat16)
    row_total = expert_ids.shape[0] * expert_ids.shape[1]
    route_ids = expert_ids.reshape(row_total, TOPK)
    route_w = route_weights.reshape(row_total, TOPK)
    matches = route_ids == roll_index
    present = jnp.any(matches, axis=1)
    row_weight = jnp.sum(jnp.where(matches, route_w, 0.0), axis=1)
    slot_of = jnp.cumsum(present.astype(jnp.int32)) - 1
    chooser = present[None, :] & (slot_of[None, :] == jnp.arange(MOSTE, dtype=jnp.int32)[:, None])
    select_half = chooser.astype(jnp.bfloat16)
    select_full = chooser.astype(jnp.float32)
    slot_weight = jnp.dot(select_full, row_weight, precision=highest)
    whole_rows = lax.all_gather(normed, "kv", axis=1, tiled=True)
    columns = select_half
    compact = jnp.dot(
        columns,
        lax.all_gather(whole_rows, "roll", axis=0, tiled=True),
        preferred_element_type=jnp.float32,
    ).astype(jnp.bfloat16)
    gate_pre = jnp.dot(compact, w_gate[0], preferred_element_type=jnp.float32)
    up_pre = jnp.dot(compact, w_up[0], preferred_element_type=jnp.float32)
    activation = (gate_pre * jax.nn.sigmoid(1.702 * gate_pre) * (up_pre + 1.0)).astype(jnp.bfloat16)
    expert_out = (
        jnp.dot(activation, w_down[0], preferred_element_type=jnp.float32) * slot_weight[:, None]
    )
    slot_sums = lax.psum_scatter(
        expert_out.astype(jnp.bfloat16), "kv", scatter_dimension=1, tiled=True
    ).astype(jnp.float32)
    columns = select_full
    expert_mix = lax.psum_scatter(
        lax.dot_general(columns, slot_sums, (((0,), (0,)), ((), ())), precision=highest),
        "roll",
        scatter_dimension=0,
        tiled=True,
    )
    return (residual_sum + expert_mix).astype(jnp.bfloat16).reshape(samp_local, step_count, -1)


def solution(mesh):
    in_specs = (
        P("roll", None, "kv"),
        P(None, "roll", "kv"),
        P("roll", None, "kv"),
        P("roll"),
        P("roll", None, "kv"),
        P("kv", None),
        P("roll", None, "kv"),
        P("kv"),
        P("roll", None, "kv"),
        P("roll", None, "kv"),
        P("roll", "kv", None),
        P(),
        P(),
    )
    out_specs = P("roll", None, "kv")
    return jax.shard_map(
        on_device, mesh=mesh, in_specs=in_specs, out_specs=out_specs, check_vma=False
    )
```

profile of v0, /device:TPU:32, one launch (start us, length us, event | category | flops | bytes accessed | tf_op | source)
XLA Modules:
  0.0 2215.5 jit_solution(90229492891172199)
XLA Ops:
  6.5 164.1 %all_gather.18 = bf16[64,4,256]{2,1,0:T(4,128)(2,1)S(1)} all-gather(bf16[1,4,256]{2,1,0:T(4,128)(2,1)} %param.15), channel_id=1, replica_groups=mesh['roll'=64,'kv'=8] {'roll'}, dimensions={0}, use_global_device_ids=true | all-gather | bytes 133120 | tf_op jit(solution)/shard_map/all_gather | solution.py:53
  175.6 1.3 dynamic-slice
  177.7 186.6 %all_gather.19 = f32[64,64,4,1,4]{1,4,3,2,0:T(4,128)S(1)} all-gather(f32[1,64,4,1,4]{1,4,3,2,0:T(4,128)S(1)} %all_gather_reshape.9), channel_id=1, replica_groups=mesh['roll'=64,'kv'=8] {'roll'}, dimensions={0}, use_global_device_ids=true | all-gather | bytes 266240 | tf_op jit(solution)/shard_map/all_gather | solution.py:13
  364.4 224.4 %all_gather.20 = f32[64,64,4,1,4]{1,4,3,2,0:T(4,128)} all-gather(f32[1,64,4,1,4]{1,4,3,2,0:T(4,128)S(1)} %bitcast.228), channel_id=1, replica_groups=mesh['roll'=64,'kv'=8] {'roll'}, dimensions={0}, use_global_device_ids=true | all-gather | bytes 266240 | tf_op jit(solution)/shard_map/all_gather | solution.py:13
  591.1 210.1 %while.19 = (s32[]{:T(128)}, f32[64,4,1,4]{0,3,2,1:T(4,128)S(1)}, f32[64,4,1,4]{0,3,2,1:T(4,128)S(1)}, f32[64,4,1,4,64]{4,3,2,1,0:T(4,128)S(1)}, f32[64,64,4,1,4...) while((s32[]{:T(128)}, f32[64,4,1,4]{0,3,2,1:T(4,128)S(1)}, ...), condition=%wide.region_3.0_spmd, body=%wide.region_2.0_spmd.sunk | while | flops 203781 | bytes 1388699 | solution.py:19
  593.2 1.2 fusion.76
  596.6 1.2 fusion.76
  599.9 1.2 fusion.76
  603.2 1.2 fusion.76
  606.6 1.2 fusion.76
  609.9 1.2 fusion.76
  613.2 1.2 fusion.76
  629.9 1.2 fusion.76
  649.9 1.2 fusion.76
  673.3 1.2 fusion.76
  693.3 1.2 fusion.76
  713.3 1.2 fusion.76
  736.6 1.2 fusion.76
  756.7 1.2 fusion.76
  776.7 1.2 fusion.76
  800.0 1.2 fusion.76
  802.9 52.3 %all-reduce = bf16[4,2880]{1,0:T(4,128)(2,1)S(1)} all-reduce(bf16[4,2880]{1,0:T(4,128)(2,1)S(1)} %convolution_convert_fusion.1), channel_id=2, replica_groups=mesh['roll'=64,'kv'=8] {'kv'}, use_global_device_ids=true, to_apply=%region_8.9.clone | all-reduce | flops 11520 | bytes 46080
  855.5 33.6 %psum.7 = f32[4]{0:T(128)S(1)} all-reduce(f32[4]{0:T(128)S(1)} %multiply_reduce_fusion), channel_id=1, replica_groups=mesh['roll'=64,'kv'=8] {'kv'}, use_global_device_ids=true, to_apply=%region_13.14 | all-reduce | flops 4 | bytes 32 | tf_op jit(solution)/shard_map/psum | solution.py:124
  889.2 39.5 %all-gather = bf16[8,360,4]{1,2,0:T(4,128)(2,1)S(1)} all-gather(bf16[1,360,4]{1,2,0:T(4,128)(2,1)S(1)} %fusion.52), channel_id=1, replica_groups=mesh['roll'=64,'kv'=8] {'kv'}, dimensions={0}, use_global_device_ids=true | all-gather | bytes 25920 | tf_op jit(solution)/shard_map/all_gather | solution.py:138
  930.9 106.3 %all-gather.7.cloned.1.call-done = bf16[64,4,2880]{2,1,0:T(4,128)(2,1)} async-done(((bf16[1,4,2880]{2,1,0:T(4,128)(2,1)}), bf16[64,4,2880]{2,1,0:T(4,128)(2,1)}) %all-gather.7.cloned.1.call-update) | async-done | bytes 1474576 | tf_op jit(solution)/shard_map/all_gather | solution.py:142
  1037.3 2.6 reshape.214
  1042.4 2.9 fusion.6
  1045.4 106.2 %all-reduce.6.cloned.1.call-done = bf16[48,2880]{1,0:T(8,128)(2,1)} async-done(((bf16[48,2880]{1,0:T(8,128)(2,1)}), bf16[48,2880]{1,0:T(8,128)(2,1)}) %all-reduce.6.cloned.1.call-update) | async-done | bytes 276496
  1151.6 1.8 fusion.33
  1153.5 1.3 dynamic-slice.4
  1155.4 1052.2 %all-reduce.8.cloned.1.call-done = f32[256,360]{1,0:T(8,128)} async-done(((f32[256,360]{1,0:T(8,128)}), f32[256,360]{1,0:T(8,128)}) %all-reduce.8.cloned.1.call-update) | async-done | bytes 368656
  2207.6 1.4 fusion.53
  (510 shorter events, 200.6 us)
Async XLA Ops:
  6.5 795.9 %copy-start = (bf16[256,2880]{0,1:T(8,128)(2,1)S(1)}, bf16[256,2880]{0,1:T(8,128)(2,1)}, u32[]{:S(2)}) copy-start(bf16[256,2880]{0,1:T(8,128)(2,1)} %param.20) | copy-start | bytes 4423684
  6.5 583.1 %all-gather.5.cloned.1.call-start = ((), (), s32[]{:S(2)}) async-start(), calls=%async_computation | async-start | bytes 34078720 | tf_op jit(solution)/shard_map/all_gather | solution.py:13
  173.0 1.0 copy-start.5
  173.9 0.8 copy-start.9
  173.9 0.9 copy-start.3
  173.9 863.4 %all-gather.7.cloned.1.call-start = ((), (), s32[]{:S(2)}) async-start(), calls=%async_computation.1 | async-start | bytes 1530880 | tf_op jit(solution)/shard_map/all_gather | solution.py:142
  801.2 54.0 %copy-start.4 = (bf16[1,4,360]{2,1,0:T(4,128)(2,1)S(1)}, bf16[1,4,360]{2,1,0:T(4,128)(2,1)}, u32[]{:S(2)}) copy-start(bf16[1,4,360]{2,1,0:T(4,128)(2,1)} %param.21) | copy-start | bytes 8644
  801.2 87.9 %copy-start.8 = (f32[360]{0:T(512)S(1)}, f32[360]{0:T(512)}, u32[]{:S(2)}) copy-start(f32[360]{0:T(512)} %param.22) | copy-start | bytes 4324
  801.4 128.1 %copy-start.6 = (f32[64,4,4]{0,2,1:T(4,128)S(1)}, f32[64,4,4]{0,2,1:T(4,128)}, u32[]{:S(2)}) copy-start(f32[64,4,4]{0,2,1:T(4,128)} %param.27) | copy-start | bytes 12292
  801.4 128.1 %copy-start.7 = (s32[64,4,4]{0,2,1:T(4,128)S(1)}, s32[64,4,4]{0,2,1:T(4,128)}, u32[]{:S(2)}) copy-start(s32[64,4,4]{0,2,1:T(4,128)} %param.26) | copy-start | bytes 12292
  929.4 222.2 %all-reduce.6.cloned.1.call-start = ((), (), s32[]{:S(2)}) async-start(), calls=%async_computation.2 | async-start | bytes 565248
  1039.9 1.2 copy-start.2
  1041.2 1.2 copy-start.1
  1045.3 1162.3 %all-reduce.8.cloned.1.call-start = ((), (), s32[]{:S(2)}) async-start(), calls=%async_computation.3 | async-start | bytes 786432
Sparse Core Ops, SparseCore 0:
  174.0 408.0 all-gather.4
  929.6 107.6 all-gather.6
  1045.5 106.0 all-reduce.5
  1154.6 1052.9 all-reduce.7
where the time goes:
time: 2220 us
  waiting for transfers between devices  1260 us (57%)
  blocking collectives  701 us (32%)
  other arithmetic  124 us (6%)
  local copies, waits for them, and re-layouts  98.2 us (4%)
    unnamed x6, waiting for transfers between devices  1160 us
    all_gather x2, blocking collectives, merged(): everything = jax.tree.map(lambda part: lax.all_gather(part, axis), x)  411 us
    all_gather x1, blocking collectives, on_device(): everyone = lax.all_gather(queries, 'roll', axis=0, tiled=True)  164 us
    all_gather x1, waiting for transfers between devices, on_device(): lax.all_gather(whole_rows, 'roll', axis=0, tiled=True)  106 us
    add x63, other arithmetic, merge_pair(): left_part[2] * left_factor[..., None]  74.7 us
    dynamic_slice x63, local copies, waits for them, and re-layouts, hop(): return combine(so_far, jax.tree.map(lambda part: part[k], everything))  68.2 us
    unnamed x1, blocking collectives  52.3 us
    mul x63, other arithmetic, merge_pair(): right_part[2] * right_factor[..., None]  45.8 us
  transfers between devices with their start and end apart: 4, of which 3 were waited for; matrix products, arithmetic and copies ran while one was open for 0% of the time, Pallas kernels for 0%

commit v1 on v0

--- a/solution.py
+++ b/solution.py
@@ -7,6 +7,11 @@
 HEAD = 64
 TOPK = 4
 MOSTE = 48
+
+
+def gather_over(x, axis, d):
+    outgoing = jnp.stack([x] * lax.axis_size(axis))
+    return jnp.concatenate(lax.all_to_all(outgoing, axis, 0, 0), axis=d)
 
 
 def merged(x, axis, combine):
@@ -50,7 +55,7 @@
     per_group = query_width // (kv_local * HEAD)
     score_scale = HEAD ** (-0.5)
     roll_index = lax.axis_index("roll")
-    everyone = lax.all_gather(queries, "roll", axis=0, tiled=True)
+    everyone = gather_over(queries, "roll", 0)
     group_size = everyone.shape[0] // prompt_count
     query_all = everyone.reshape(prompt_count, group_size, step_count, kv_local, per_group, HEAD)
     prompt_blocks = prompt_cache.reshape(prompt_count, prompt_local, kv_local, 2, HEAD)

time: 2220 us -> 2100 us (0.946)
  blocking collectives: 701 us -> 515 us
  waiting for transfers between devices: 1260 us -> 1300 us
    all_gather x1 -> x0, blocking collectives: 164 us -> none  [on_device(): everyone = lax.all_gather(queries, 'roll', axis=0, tiled=True)]
    all_gather x2, blocking collectives: 411 us -> 362 us  [merged(): everything = jax.tree.map(lambda part: lax.all_gather(part, axis), x)]
    unnamed x1, blocking collectives: 52.3 us -> 81.5 us
    all_gather x1, waiting for transfers between devices: 0.01 us -> 24.3 us  [merged(): everything = jax.tree.map(lambda part: lax.all_gather(part, axis), x)]
  transfers between devices with their start and end apart: 4 -> 5, of which waited for: 3 -> 5; matrix products, arithmetic and copies ran while one was open for 0% -> 0% of each run, Pallas kernels for 0% -> 0%
where the time goes in v1:
time: 2100 us; the launch traced here: 2090 us
  waiting for transfers between devices  1300 us (62%)
  blocking collectives  515 us (25%)
  other arithmetic  125 us (6%)
  local copies, waits for them, and re-layouts  99.7 us (5%)
    unnamed x6, waiting for transfers between devices  1160 us
    all_gather x2, blocking collectives, merged(): everything = jax.tree.map(lambda part: lax.all_gather(part, axis), x)  362 us
    all_gather x1, waiting for transfers between devices, on_device(): lax.all_gather(whole_rows, 'roll', axis=0, tiled=True)  101 us
    unnamed x1, blocking collectives  81.5 us
    add x63, other arithmetic, merge_pair(): left_part[2] * left_factor[..., None]  75 us
    dynamic_slice x63, local copies, waits for them, and re-layouts, hop(): return combine(so_far, jax.tree.map(lambda part: part[k], everything))  68.2 us
    mul x63, other arithmetic, merge_pair(): right_part[2] * right_factor[..., None]  45.8 us
  transfers between devices with their start and end apart: 5, of which 5 were waited for; matrix products, arithmetic and copies ran while one was open for 0% of the time, Pallas kernels for 0%

profile of v1, /device:TPU:32, one launch (start us, length us, event | category | flops | bytes accessed | tf_op | source)
XLA Modules:
  0.0 2091.7 jit_solution(7596711583473457345)
XLA Ops:
  6.5 1.5 stack.2
  8.0 20.3 all-to-all-start
  29.4 20.2 all-to-all-done
  53.0 1.3 dynamic-slice
  56.0 175.0 %all_gather.15 = f32[64,64,4,1,4]{1,4,3,2,0:T(4,128)S(1)} all-gather(f32[1,64,4,1,4]{1,4,3,2,0:T(4,128)S(1)} %all_gather_reshape.9), channel_id=1, replica_groups=mesh['roll'=64,'kv'=8] {'roll'}, dimensions={0}, use_global_device_ids=true | all-gather | bytes 266240 | tf_op jit(solution)/shard_map/all_gather | solution.py:18
  231.0 187.0 %all_gather.16 = f32[64,64,4,1,4]{1,4,3,2,0:T(4,128)} all-gather(f32[1,64,4,1,4]{1,4,3,2,0:T(4,128)S(1)} %bitcast.229), channel_id=1, replica_groups=mesh['roll'=64,'kv'=8] {'roll'}, dimensions={0}, use_global_device_ids=true | all-gather | bytes 266240 | tf_op jit(solution)/shard_map/all_gather | solution.py:18
  418.8 24.3 %all-gather.5.cloned.1.call-done = f32[64,64,4,1,4,64]{5,1,4,3,2,0:T(8,128)} async-done(((f32[1,64,4,1,4,64]{5,1,4,3,2,0:T(8,128)}), f32[64,64,4,1,4,64]{5,1,4,3,2,0:T(8,128)}) %all-gather.5.cloned.1.call-update) | async-done | bytes 16777232 | tf_op jit(solution)/shard_map/all_gather | solution.py:18
  444.5 210.5 %while.19 = (s32[]{:T(128)}, f32[64,4,1,4]{0,3,2,1:T(4,128)S(1)}, f32[64,4,1,4]{0,3,2,1:T(4,128)S(1)}, f32[64,4,1,4,64]{4,3,2,1,0:T(4,128)S(1)}, f32[64,64,4,1,4...) while((s32[]{:T(128)}, f32[64,4,1,4]{0,3,2,1:T(4,128)S(1)}, ...), condition=%wide.region_3.0_spmd, body=%wide.region_2.0_spmd.sunk | while | flops 203781 | bytes 1388699 | solution.py:24
  456.6 1.2 fusion.76
  466.7 1.2 fusion.76
  476.7 1.2 fusion.76
  486.7 1.2 fusion.76
  496.7 1.2 fusion.76
  506.7 1.2 fusion.76
  520.1 1.2 fusion.76
  530.1 1.2 fusion.76
  540.1 1.2 fusion.76
  550.2 1.2 fusion.76
  560.2 1.2 fusion.76
  570.2 1.2 fusion.76
  583.6 1.2 fusion.76
  656.6 81.5 %all-reduce = bf16[4,2880]{1,0:T(4,128)(2,1)S(1)} all-reduce(bf16[4,2880]{1,0:T(4,128)(2,1)S(1)} %convolution_convert_fusion.1), channel_id=2, replica_groups=mesh['roll'=64,'kv'=8] {'kv'}, use_global_device_ids=true, to_apply=%region_8.9.clone | all-reduce | flops 11520 | bytes 46080
  738.3 31.8 %psum.7 = f32[4]{0:T(128)S(1)} all-reduce(f32[4]{0:T(128)S(1)} %multiply_reduce_fusion), channel_id=1, replica_groups=mesh['roll'=64,'kv'=8] {'kv'}, use_global_device_ids=true, to_apply=%region_13.14 | all-reduce | flops 4 | bytes 32 | tf_op jit(solution)/shard_map/psum | solution.py:129
  770.2 39.5 %all-gather = bf16[8,360,4]{1,2,0:T(4,128)(2,1)S(1)} all-gather(bf16[1,360,4]{1,2,0:T(4,128)(2,1)S(1)} %fusion.52), channel_id=1, replica_groups=mesh['roll'=64,'kv'=8] {'kv'}, dimensions={0}, use_global_device_ids=true | all-gather | bytes 25920 | tf_op jit(solution)/shard_map/all_gather | solution.py:143
  812.0 101.5 %all-gather.7.cloned.1.call-done = bf16[64,4,2880]{2,1,0:T(4,128)(2,1)} async-done(((bf16[1,4,2880]{2,1,0:T(4,128)(2,1)}), bf16[64,4,2880]{2,1,0:T(4,128)(2,1)}) %all-gather.7.cloned.1.call-update) | async-done | bytes 1474576 | tf_op jit(solution)/shard_map/all_gather | solution.py:147
  913.5 2.6 reshape.216
  918.6 2.9 fusion.6
  921.6 106.2 %all-reduce.6.cloned.1.call-done = bf16[48,2880]{1,0:T(8,128)(2,1)} async-done(((bf16[48,2880]{1,0:T(8,128)(2,1)}), bf16[48,2880]{1,0:T(8,128)(2,1)}) %all-reduce.6.cloned.1.call-update) | async-done | bytes 276496
  1027.8 1.8 fusion.33
  1029.7 1.3 dynamic-slice.4
  1031.6 1052.2 %all-reduce.8.cloned.1.call-done = f32[256,360]{1,0:T(8,128)} async-done(((f32[256,360]{1,0:T(8,128)}), f32[256,360]{1,0:T(8,128)}) %all-reduce.8.cloned.1.call-update) | async-done | bytes 368656
  2083.8 1.4 fusion.53
  (512 shorter events, 204.4 us)
Async XLA Ops:
  6.5 649.6 %copy-start = (bf16[256,2880]{0,1:T(8,128)(2,1)S(1)}, bf16[256,2880]{0,1:T(8,128)(2,1)}, u32[]{:S(2)}) copy-start(bf16[256,2880]{0,1:T(8,128)(2,1)} %param.20) | copy-start | bytes 4423684
  8.0 41.7 %all-to-all-start = ((bf16[64,1,4,256]{3,2,1,0:T(4,128)(2,1)}), bf16[64,1,4,256]{3,2,1,0:T(4,128)(2,1)S(1)}, u32[]{:S(2)}, u32[]{:S(2)}) async-start(bf16[64,1,4,256]{3,2,1,0:T(4,128)(2,1)} %stack.2), calls=%async_computation | async-start | bytes 262144 | tf_op jit(solution)/shard_map/all_to_all | solution.py:14
  28.3 414.7 %all-gather.5.cloned.1.call-start = ((), (), s32[]{:S(2)}) async-start(), calls=%async_computation.1 | async-start | bytes 34078720 | tf_op jit(solution)/shard_map/all_gather | solution.py:18
  51.0 1.0 copy-start.5
  51.0 1.1 copy-start.9
  51.0 1.1 copy-start.3
  51.9 861.6 %all-gather.7.cloned.1.call-start = ((), (), s32[]{:S(2)}) async-start(), calls=%async_computation.2 | async-start | bytes 1530880 | tf_op jit(solution)/shard_map/all_gather | solution.py:147
  654.9 83.2 %copy-start.4 = (bf16[1,4,360]{2,1,0:T(4,128)(2,1)S(1)}, bf16[1,4,360]{2,1,0:T(4,128)(2,1)}, u32[]{:S(2)}) copy-start(bf16[1,4,360]{2,1,0:T(4,128)(2,1)} %param.21) | copy-start | bytes 8644
  654.9 115.2 %copy-start.8 = (f32[360]{0:T(512)S(1)}, f32[360]{0:T(512)}, u32[]{:S(2)}) copy-start(f32[360]{0:T(512)} %param.22) | copy-start | bytes 4324
  655.1 155.5 %copy-start.6 = (f32[64,4,4]{0,2,1:T(4,128)S(1)}, f32[64,4,4]{0,2,1:T(4,128)}, u32[]{:S(2)}) copy-start(f32[64,4,4]{0,2,1:T(4,128)} %param.27) | copy-start | bytes 12292
  655.1 155.5 %copy-start.7 = (s32[64,4,4]{0,2,1:T(4,128)S(1)}, s32[64,4,4]{0,2,1:T(4,128)}, u32[]{:S(2)}) copy-start(s32[64,4,4]{0,2,1:T(4,128)} %param.26) | copy-start | bytes 12292
  810.5 217.3 %all-reduce.6.cloned.1.call-start = ((), (), s32[]{:S(2)}) async-start(), calls=%async_computation.3 | async-start | bytes 565248
  916.2 1.2 copy-start.2
  917.4 1.2 copy-start.1
  921.6 1162.3 %all-reduce.8.cloned.1.call-start = ((), (), s32[]{:S(2)}) async-start(), calls=%async_computation.4 | async-start | bytes 786432
Sparse Core Ops, SparseCore 0:
  52.1 390.9 all-gather.4
  810.6 102.8 all-gather.6
  921.7 106.0 all-reduce.5
  1030.9 1052.9 all-reduce.7
